TPU v7x, 32 devices: a whole 2x2x4 slice. The times are simulated.
32 devices in a mesh: grp: 4 (over z), row: 8 (over y, x, core).
Axes of the slice: x: 2, y: 2, z: 4, core: 2. Of those that a mesh axis runs over, the one named last changes fastest.
Arguments:
- basis: float32 [8192, 1024], P(('grp', 'row')), may hold values from -40 to 40
- block: float32 [8192, 512], P(('grp', 'row')), may hold values from -600 to 600
- counts: int32 [4, 8], P('grp', 'row'), may hold values from 128 to 256, as said below
Outputs:
- new_block: float32 [8192, 512], P(('grp', 'row'))
- factor: float32 [512, 512], replicated
Inputs may be any that keep to these rules, and one draw needn't show every extreme that they name: `counts`: each device's live rows are a multiple of 128, at most 256; one device holds exactly 256.
All inputs are finite; a program needn't handle non-finite values.
Results may differ from a plain program's by a relative error of at most 0.0003.
Values sent between devices are 32-bit elements; how exact they have to be, the bound alone decides.
A program may use at most 64 MiB of HBM per device.

v0:
```python
import functools

import jax
import jax.numpy as jnp
from jax import lax
from jax.experimental import pallas as pl
from jax.experimental.pallas import tpu as pltpu
from jax.sharding import PartitionSpec as P

HIGHEST = lax.Precision.HIGHEST
MESH = pl.DeviceIdType.MESH
TILE = 128


def transposed_product(left, right):
    return lax.dot_general(
        left,
        right,
        (((0,), (0,)), ((), ())),
        precision=HIGHEST,
        preferred_element_type=jnp.float32,
    )


def matrix_product(left, right):
    return jnp.dot(left, right, precision=HIGHEST, preferred_element_type=jnp.float32)


def column_split(rows, cols, first, second):
    split = 1
    while split <= second and cols % (split * TILE) == 0:
        if rows % first == 0 and (rows // first) % (second // split * 8) == 0:
            return split
        split *= 2
    return None


def plan_parts(rows, cols, sizes):
    half = cols // 2
    parts = []
    for start, order in ((0, ("row", "grp")), (half, ("grp", "row"))):
        parts.append((start, half, order, column_split(rows, half, sizes[order[0]], sizes[order[1]])))
    if all(part[3] is not None for part in parts):
        return parts
    order = ("row", "grp")
    split = column_split(rows, cols, sizes["row"], sizes["grp"])
    assert split is not None
    return [(0, cols, order, split)]


def all_reduce_kernel(parts, sizes, x_ref, out_ref, *scratch):
    rows = x_ref.shape[0]
    me = {axis: lax.axis_index(axis) for axis in sizes}

    def ahead(axis, k):
        return lax.rem(me[axis] + k, sizes[axis])

    barrier = pltpu.get_barrier_semaphore()
    for axis in sizes:
        for k in range(1, sizes[axis]):
            pl.semaphore_signal(barrier, inc=1, device_id={axis: ahead(axis, k)}, device_id_type=MESH)
    pl.semaphore_wait(barrier, sum(size - 1 for size in sizes.values()))

    groups = [scratch[7 * i : 7 * i + 7] for i in range(len(parts))]

    def first_chunk(part, index):
        start, width, order, _ = part
        height = rows // sizes[order[0]]
        return pl.ds(pl.multiple_of(index * height, 8), height), pl.ds(start, width)

    def second_chunk(part, index):
        start, width, order, split = part
        height = rows // sizes[order[0]] // (sizes[order[1]] // split)
        piece = width // split
        if split == 1:
            return pl.multiple_of(index * height, 8), height, start, 0, piece
        row = pl.multiple_of(lax.div(index, split) * height, 8)
        offset = pl.multiple_of(lax.rem(index, split) * piece, TILE)
        return row, height, start + offset, offset, piece

    def send(source, target, send_sem, recv_sem, axis, k):
        copy = pltpu.make_async_remote_copy(
            src_ref=source,
            dst_ref=target,
            send_sem=send_sem,
            recv_sem=recv_sem,
            device_id={axis: ahead(axis, k)},
            device_id_type=MESH,
        )
        copy.start()
        return copy

    sent = []
    stage = [[] for _ in parts]
    most = max(sizes.values())
    for k in range(1, most):
        for i, part in enumerate(parts):
            axis = part[2][0]
            if k < sizes[axis]:
                held, _, _, sends, recvs, _, _ = groups[i]
                rs, cs = first_chunk(part, ahead(axis, k))
                stage[i].append(
                    send(x_ref.at[rs, cs], held.at[k - 1], sends.at[k - 1], recvs.at[k - 1], axis, k)
                )
    for i, part in enumerate(parts):
        axis, other = part[2]
        held, partial, held_second, _, _, sends, recvs = groups[i]
        for copy in stage[i]:
            copy.wait_recv()
        rs, cs = first_chunk(part, me[axis])
        total = x_ref[rs, cs]
        for k in range(sizes[axis] - 1):
            total = total + held[k]
        partial[...] = total
        sent += stage[i]
        stage[i] = []
        for k in range(1, sizes[other]):
            row, height, _, offset, piece = second_chunk(part, ahead(other, k))
            stage[i].append(
                send(
                    partial.at[pl.ds(row, height), pl.ds(offset, piece)],
                    held_second.at[k - 1],
                    sends.at[0, k - 1],
                    recvs.at[0, k - 1],
                    other,
                    k,
                )
            )
    for i, part in enumerate(parts):
        axis, other = part[2]
        _, partial, held_second, _, _, sends, recvs = groups[i]
        for copy in stage[i]:
            copy.wait_recv()
        row, height, column, offset, piece = second_chunk(part, me[other])
        total = partial[pl.ds(row, height), pl.ds(offset, piece)]
        for k in range(sizes[other] - 1):
            total = total + held_second[k]
        base = me[axis] * (rows // sizes[axis])
        place = out_ref.at[pl.ds(pl.multiple_of(base + row, 8), height), pl.ds(column, piece)]
        place[...] = total
        sent += stage[i]
        stage[i] = []
        for k in range(1, sizes[other]):
            stage[i].append(send(place, place, sends.at[1, k - 1], recvs.at[1, k - 1], other, k))
    for i, part in enumerate(parts):
        axis, _ = part[2]
        final_sends, final_recvs = scratch[7 * len(parts) + 2 * i : 7 * len(parts) + 2 * i + 2]
        for copy in stage[i]:
            copy.wait_recv()
        sent += stage[i]
        stage[i] = []
        rs, cs = first_chunk(part, me[axis])
        place = out_ref.at[rs, cs]
        for k in range(1, sizes[axis]):
            stage[i].append(send(place, place, final_sends.at[k - 1], final_recvs.at[k - 1], axis, k))
    for i in range(len(parts)):
        for copy in stage[i]:
            copy.wait_recv()
        sent += stage[i]
    for copy in sent:
        copy.wait_send()


def all_reduce(x, collective_id):
    rows, cols = x.shape
    sizes = {axis: lax.axis_size(axis) for axis in ("grp", "row")}
    parts = plan_parts(rows, cols, sizes)
    scratch = []
    for _, width, (axis, other), split in parts:
        height = rows // sizes[axis]
        scratch += [
            pltpu.VMEM((sizes[axis] - 1, height, width), jnp.float32),
            pltpu.VMEM((height, width), jnp.float32),
            pltpu.VMEM((sizes[other] - 1, height // (sizes[other] // split), width // split), jnp.float32),
            pltpu.SemaphoreType.DMA((sizes[axis] - 1,)),
            pltpu.SemaphoreType.DMA((sizes[axis] - 1,)),
            pltpu.SemaphoreType.DMA((2, sizes[other] - 1)),
            pltpu.SemaphoreType.DMA((2, sizes[other] - 1)),
        ]
    for _, _, (axis, _), _ in parts:
        scratch += [pltpu.SemaphoreType.DMA((sizes[axis] - 1,))] * 2
    return pl.pallas_call(
        functools.partial(all_reduce_kernel, parts, sizes),
        out_shape=jax.ShapeDtypeStruct((rows, cols), jnp.float32),
        in_specs=[pl.BlockSpec(memory_space=pltpu.VMEM)],
        out_specs=pl.BlockSpec(memory_space=pltpu.VMEM),
        scratch_shapes=scratch,
        compiler_params=pltpu.CompilerParams(collective_id=collective_id, has_side_effects=True),
        name=f"all_reduce_{collective_id}",
    )(x)


def eliminate(block):
    size = block.shape[0]
    count = size // 8
    sub = lax.broadcasted_iota(jnp.int32, (8, size), 0)
    lane = lax.broadcasted_iota(jnp.int32, (8, size), 1)
    left = [block[8 * b : 8 * b + 8] for b in range(count)]
    right = [(lane == sub + 8 * b).astype(jnp.float32) for b in range(count)]
    for j in range(size):
        home, inner = divmod(j, 8)
        row = left[home][inner : inner + 1]
        companion = right[home][inner : inner + 1]
        inverse = 1.0 / row[:, j : j + 1]
        row = row * inverse
        companion = companion * inverse
        for b in range(home, count):
            if b == home and inner == 7:
                continue
            factor = jnp.broadcast_to(left[b][:, j : j + 1], (8, size))
            if b == home:
                factor = jnp.where(sub > inner, factor, 0.0)
            left[b] = left[b] - factor * row
            right[b] = right[b] - factor * companion
    upper, inverted = [], []
    for b in range(count):
        diagonal = jnp.sum(jnp.where(lane == sub + 8 * b, left[b], 0.0), axis=1, keepdims=True)
        root = 1.0 / jnp.sqrt(diagonal)
        upper.append(jnp.where(lane >= sub + 8 * b, left[b] * root, 0.0))
        inverted.append(jnp.where(lane <= sub + 8 * b, right[b] * root, 0.0))
    return jnp.concatenate(upper, axis=0), jnp.concatenate(inverted, axis=0)


def factor_kernel(gram_ref, residual_ref, new_ref, factor_ref, work, rest):
    size = gram_ref.shape[0]
    work[...] = gram_ref[...]
    rest[...] = residual_ref[...]

    def step(index, carry):
        window = pl.ds(pl.multiple_of(index * TILE, TILE), TILE)
        upper, inverted = eliminate(work[window, window])
        panel = matrix_product(inverted, work[window, :])
        column = lax.broadcasted_iota(jnp.int32, (TILE, size), 1)
        panel = jnp.where(column >= (index + 1) * TILE, panel, 0.0)
        factor_ref[window, :] = panel
        factor_ref[window, window] = upper
        work[...] -= transposed_product(panel, panel)
        solved = lax.dot_general(
            rest[:, window],
            inverted,
            (((1,), (1,)), ((), ())),
            precision=HIGHEST,
            preferred_element_type=jnp.float32,
        )
        new_ref[:, window] = solved
        rest[...] -= matrix_product(solved, panel)
        return carry

    lax.fori_loop(0, size // TILE, step, 0)


def factor_and_solve(gram, residual):
    vmem = pl.BlockSpec(memory_space=pltpu.VMEM)
    return pl.pallas_call(
        factor_kernel,
        out_shape=(
            jax.ShapeDtypeStruct(residual.shape, jnp.float32),
            jax.ShapeDtypeStruct(gram.shape, jnp.float32),
        ),
        in_specs=[vmem, vmem],
        out_specs=(vmem, vmem),
        scratch_shapes=[pltpu.VMEM(gram.shape, jnp.float32), pltpu.VMEM(residual.shape, jnp.float32)],
        name="factor_and_solve",
    )(gram, residual)


def body(basis, block, counts):
    row_slots = block.shape[0]
    devices = lax.axis_size("grp") * lax.axis_size("row")
    weight = 1.0 / (row_slots * devices)
    live = (lax.iota(jnp.int32, row_slots) < counts[0, 0]).astype(jnp.float32)[:, None]
    basis_live = basis * live
    block_live = block * live
    coeffs = all_reduce(transposed_product(basis_live, block_live) * weight, 0)
    first_pass = block_live - matrix_product(basis_live, coeffs)
    correction = all_reduce(transposed_product(basis_live, first_pass) * weight, 1)
    residual = first_pass - matrix_product(basis_live, correction)
    gram = all_reduce(transposed_product(residual, residual) * weight, 2)
    return factor_and_solve(gram, residual)


def solution(mesh):
    placed = (P(("grp", "row"), None), P(("grp", "row"), None), P("grp", "row"))
    return jax.shard_map(
        body, mesh=mesh, in_specs=placed, out_specs=(P(("grp", "row"), None), P()), check_vma=False
    )
```

profile of v0, /device:TPU:1, one launch (start us, length us, event | category | flops | bytes accessed | tf_op | source)
XLA Modules:
  0.0 238.9 jit_solution(9111786552993633946)
XLA Ops:
  1.3 4.7 %convolution_multiply_fusion.1.x_ref = f32[1024,512]{1,0:T(8,128)} fusion(f32[256,1024]{1,0:T(8,128)} %param.3, f32[256]{0:T(256)S(1)} %compare_convert_fusion, f32[256,512]{1,0:T(8,128)} %param.4), kind=kOutput, calls=%fused_computation.1 | convolution fusion | flops 1611530240 | bytes 3671040 | tf_op jit(solution)/shard_map/dot_general | solution.py:16
  6.0 0.0 copy-start
  6.0 0.0 copy-start.2
  6.0 58.3 %all_reduce_0.1 = f32[1024,512]{1,0:T(8,128)} custom-call(f32[1024,512]{1,0:T(8,128)} %convolution_multiply_fusion.1.x_ref), custom_call_target="tpu_custom_call" | custom-call | tf_op jit(solution)/shard_map/all_reduce_0/pallas_call | solution.py:182
  64.3 0.0 copy-done
  64.3 0.0 copy-done.2
  64.4 3.6 %convolution_subtract_fusion.1 = f32[256,512]{1,0:T(8,128)S(1)} fusion(f32[1024,512]{1,0:T(8,128)} %all_reduce_0.1, f32[256,1024]{1,0:T(8,128)S(1)} %copy-done, f32[256]{0:T(256)S(1)} %compare_convert_fusion, f32[256,512]{1,0:T(8,128)S(1)} %copy-done.2), kind=kOutput, calls=%fused_computation.4 | convolution fusion | flops 1611137024 | bytes 4195328 | tf_op jit(solution)/shard_map/dot_general | solution.py:26
  67.9 3.3 %convolution_multiply_fusion.x_ref = f32[1024,512]{1,0:T(8,128)} fusion(f32[256,512]{1,0:T(8,128)S(1)} %convolution_subtract_fusion.1, f32[256,1024]{1,0:T(8,128)S(1)} %copy-done, f32[256]{0:T(256)S(1)} %compare_convert_fusion), kind=kOutput, calls=%fused_computation | convolution fusion | flops 1611399168 | bytes 3671040 | tf_op jit(solution)/shard_map/dot_general | solution.py:16
  71.2 65.7 %all_reduce_1.1 = f32[1024,512]{1,0:T(8,128)} custom-call(f32[1024,512]{1,0:T(8,128)} %convolution_multiply_fusion.x_ref), custom_call_target="tpu_custom_call" | custom-call | tf_op jit(solution)/shard_map/all_reduce_1/pallas_call | solution.py:182
  136.9 3.6 %convolution_subtract_fusion.residual_ref = f32[256,512]{1,0:T(8,128)S(1)} fusion(f32[256,512]{1,0:T(8,128)S(1)} %convolution_subtract_fusion.1, f32[1024,512]{1,0:T(8,128)} %all_reduce_1.1, f32[256,1024]{1,0:T(8,128)S(1)} %copy-done, f32[256]{0:T(256)S(1)} %compare_convert_fusion), kind=kOutput, calls=%fused_computation.3 | convolution fusion | flops 1611005952 | bytes 4195328 | tf_op jit(solution)/shard_map/dot_general | solution.py:26
  140.4 0.0 copy-start.1
  140.5 2.0 convolution_multiply_fusion.2.x_ref
  142.5 43.7 %all_reduce_2.1.gram_ref = f32[512,512]{1,0:T(8,128)} custom-call(f32[512,512]{1,0:T(8,128)} %convolution_multiply_fusion.2.x_ref), custom_call_target="tpu_custom_call" | custom-call | tf_op jit(solution)/shard_map/all_reduce_2/pallas_call | solution.py:182
  186.2 0.0 copy-done.1
  186.2 52.8 %factor_and_solve.1 = (f32[256,512]{1,0:T(8,128)}, f32[512,512]{1,0:T(8,128)}) custom-call(f32[512,512]{1,0:T(8,128)} %all_reduce_2.1.gram_ref, f32[256,512]{1,0:T(8,128)} %copy-done.1), custom_call_target="tpu_custom_call" | custom-call | tf_op jit(solution)/shard_map/factor_and_solve/pallas_call | solution.py:254
  (1 shorter events, 0.0 us)
Async XLA Ops:
  6.0 58.4 %copy-start = (f32[256,1024]{1,0:T(8,128)S(1)}, f32[256,1024]{1,0:T(8,128)}, u32[]{:S(2)}) copy-start(f32[256,1024]{1,0:T(8,128)} %param.3) | copy-start | bytes 3145732
  6.0 58.4 %copy-start.2 = (f32[256,512]{1,0:T(8,128)S(1)}, f32[256,512]{1,0:T(8,128)}, u32[]{:S(2)}) copy-start(f32[256,512]{1,0:T(8,128)} %param.4) | copy-start | bytes 1572868
  140.4 45.7 %copy-start.1 = (f32[256,512]{1,0:T(8,128)}, f32[256,512]{1,0:T(8,128)S(1)}, u32[]{:S(2)}) copy-start(f32[256,512]{1,0:T(8,128)S(1)} %convolution_subtract_fusion.residual_ref) | copy-start | bytes 1572868
where the time goes:
time: 242 us; the launch traced here: 239 us
  Pallas kernels  220 us (91%)
  matrix products  17.1 us (7%)
    pallas_call x3, Pallas kernels, all_reduce(): pl.pallas_call(functools.partial(all_reduce_kernel, parts, sizes), out_sh...  168 us
    pallas_call x1, Pallas kernels, factor_and_solve(): pl.pallas_call(factor_kernel, out_shape=(jax.ShapeDtypeStruct(residual.sh...  52.8 us
    dot_general x3, matrix products, transposed_product(): lax.dot_general(left, right, (((0,), (0,)), ((), ())), precision=HIGHEST,...  9.96 us
    dot_general x2, matrix products, matrix_product(): jnp.dot(left, right, precision=HIGHEST, preferred_element_type=jnp.float32)  7.12 us

commit v1 on v0

v1 whole, which is shorter than its diff:
```python
import functools
import math

import jax
import jax.numpy as jnp
from jax import lax
from jax.experimental import pallas as pl
from jax.experimental.pallas import tpu as pltpu
from jax.sharding import PartitionSpec as P

HIGHEST = lax.Precision.HIGHEST
MESH = pl.DeviceIdType.MESH
TILE = 128


def transposed_product(left, right):
    return lax.dot_general(
        left,
        right,
        (((0,), (0,)), ((), ())),
        precision=HIGHEST,
        preferred_element_type=jnp.float32,
    )


def matrix_product(left, right):
    return jnp.dot(left, right, precision=HIGHEST, preferred_element_type=jnp.float32)


def plane_sides(chips):
    side = math.isqrt(chips)
    while chips % side:
        side -= 1
    return chips // side, side


class Piece:
    def __init__(self, tiles, order, chips):
        self.used = tiles
        self.tiles = -(-tiles // chips) * chips
        self.order = order


def make_plan(basis_columns, block_columns, sizes):
    chips = sizes["x"] * sizes["y"] * sizes["z"]
    block = basis_columns // 4
    half = block_columns // 2
    square = block * block // 1024
    corner = half * half // 1024
    forward, backward = ("x", "y", "z"), ("y", "x", "z")
    basis_gram = [
        Piece(2 * (square - square // 4), forward, chips),
        Piece(square, backward, chips),
        Piece(square, backward, chips),
        Piece(square, forward, chips),
    ]
    coeffs = [Piece(block * half // 1024, (forward, backward)[i % 2], chips) for i in range(4)]
    gram = [Piece(corner - corner // 4, forward, chips), Piece(corner // 2, backward, chips)]
    place = dict(copy=0, source=0, held=0, partial=0)
    for group in (basis_gram, coeffs, gram):
        offset = 0
        for piece in group:
            piece.offset = offset
            offset += piece.tiles
            piece.source = place["source"]
            place["source"] += piece.tiles
            piece.stages = []
            size = piece.tiles
            for axis in piece.order:
                count = sizes[axis]
                size //= count
                stage = dict(axis=axis, size=size, held=place["held"], partial=place["partial"])
                stage["scatter"] = place["copy"]
                stage["gather"] = place["copy"] + count - 1
                place["copy"] += 2 * (count - 1)
                place["held"] += (count - 1) * size
                place["partial"] += size
                piece.stages.append(stage)
            piece.partner = place["copy"]
            place["copy"] += 1
    return basis_gram, coeffs, gram, place


def pieces_to_tiles(value):
    rows, cols = value.shape
    return [value[:, i : i + TILE].reshape(rows // 8, 8, TILE) for i in range(0, cols, TILE)]


def orthogonalize_kernel(
    plan,
    sizes,
    weight,
    counts_ref,
    basis_ref,
    block_ref,
    residual_ref,
    gram_ref,
    basis_all,
    block_half,
    block_send,
    source,
    held,
    partial,
    basis_gram_tiles,
    coeffs_tiles,
    gram_tiles,
    operator,
    correction,
    residual,
    send_sem,
    recv_sem,
    extra_send,
    extra_recv,
):
    basis_gram, coeffs, gram, _ = plan
    slots = basis_ref.shape[0]
    columns = basis_ref.shape[1]
    half = block_ref.shape[1] // 2
    block = columns // 4

    row = lax.axis_index("row")
    core = lax.rem(row, 2)
    chip = lax.div(row, 2)
    me = {"x": lax.rem(chip, sizes["x"]), "y": lax.div(chip, sizes["x"]), "z": lax.axis_index("grp")}
    partner = {"row": row + 1 - 2 * core}

    def peer(axis, k):
        other = lax.rem(me[axis] + k, sizes[axis])
        if axis == "z":
            return {"grp": other}
        x, y = (other, me["y"]) if axis == "x" else (me["x"], other)
        return {"row": (y * sizes["x"] + x) * 2 + core}

    barrier = pltpu.get_barrier_semaphore()
    pl.semaphore_signal(barrier, inc=1, device_id=partner, device_id_type=MESH)
    for axis in sizes:
        for k in range(1, sizes[axis]):
            pl.semaphore_signal(barrier, inc=1, device_id=peer(axis, k), device_id_type=MESH)
    sent = []

    def start(source_ref, target_ref, sends, recvs, device):
        copy = pltpu.make_async_remote_copy(
            src_ref=source_ref,
            dst_ref=target_ref,
            send_sem=sends,
            recv_sem=recvs,
            device_id=device,
            device_id_type=MESH,
        )
        copy.start()
        sent.append(copy)
        return copy

    live = lax.broadcasted_iota(jnp.int32, (slots, 1), 0) < counts_ref[0, 0]
    mine = pl.ds(pl.multiple_of(core * slots, 8), slots)
    near = pl.ds(pl.multiple_of(core * half, TILE), half)
    far = pl.ds(pl.multiple_of((1 - core) * half, TILE), half)
    basis_all[mine, :] = jnp.where(live, basis_ref[...], 0.0)
    block_send[...] = jnp.where(live, block_ref[:, far], 0.0)
    block_half[mine, :] = jnp.where(live, block_ref[:, near], 0.0)
    pl.semaphore_wait(barrier, 1 + sum(size - 1 for size in sizes.values()))
    shared = [
        start(basis_all.at[mine], basis_all.at[mine], extra_send.at[0], extra_recv.at[0], partner),
        start(block_send, block_half.at[mine], extra_send.at[1], extra_recv.at[1], partner),
    ]

    def position(piece, depth):
        offset = 0
        for stage in piece.stages[:depth]:
            offset = offset + me[stage["axis"]] * stage["size"]
        return offset

    def scatter(piece, depth):
        stage = piece.stages[depth]
        axis, size = stage["axis"], stage["size"]
        if depth == 0:
            base, ref = piece.source, source
        else:
            base, ref = piece.stages[depth - 1]["partial"], partial
        piece.waiting = []
        for k in range(1, sizes[axis]):
            chunk = lax.rem(me[axis] + k, sizes[axis]) * size
            index = stage["scatter"] + k - 1
            piece.waiting.append(
                start(
                    ref.at[pl.ds(base + chunk, size)],
                    held.at[pl.ds(stage["held"] + (k - 1) * size, size)],
                    send_sem.at[index],
                    recv_sem.at[index],
                    peer(axis, k),
                )
            )

    def reduced(piece, depth):
        stage = piece.stages[depth]
        axis, size = stage["axis"], stage["size"]
        if depth == 0:
            base, ref = piece.source, source
        else:
            base, ref = piece.stages[depth - 1]["partial"], partial
        for copy in piece.waiting:
            copy.wait_recv()
        total = ref[pl.ds(base + me[axis] * size, size)]
        for k in range(sizes[axis] - 1):
            total = total + held[pl.ds(stage["held"] + k * size, size)]
        return total

    def gather(piece, depth):
        stage = piece.stages[depth]
        axis = stage["axis"]
        place = piece.out.at[pl.ds(piece.offset + position(piece, depth + 1), stage["size"])]
        piece.waiting = []
        for k in range(1, sizes[axis]):
            index = stage["gather"] + k - 1
            piece.waiting.append(start(place, place, send_sem.at[index], recv_sem.at[index], peer(axis, k)))

    def advance(piece, step):
        if step == 0:
            blocks = piece.produce()
            offset = piece.source
            for value in blocks:
                source[pl.ds(offset, value.shape[0])] = value
                offset += value.shape[0]
            if piece.used < piece.tiles:
                source[pl.ds(offset, piece.tiles - piece.used)] = jnp.zeros(
                    (piece.tiles - piece.used, 8, TILE), jnp.float32
                )
            scatter(piece, 0)
        elif step < 3:
            stage = piece.stages[step - 1]
            partial[pl.ds(stage["partial"], stage["size"])] = reduced(piece, step - 1)
            scatter(piece, step)
        elif step == 3:
            size = piece.stages[2]["size"]
            piece.out[pl.ds(piece.offset + position(piece, 3), size)] = reduced(piece, 2)
            gather(piece, 2)
        elif step < 6:
            for copy in piece.waiting:
                copy.wait_recv()
            gather(piece, 5 - step)
        elif step == 6:
            for copy in piece.waiting:
                copy.wait_recv()
            if piece.shared:
                place = piece.out.at[pl.ds(piece.offset, piece.tiles)]
                index = piece.partner
                piece.waiting = [start(place, place, send_sem.at[index], recv_sem.at[index], partner)]
            else:
                piece.consume()
        elif step == 7 and piece.shared:
            for copy in piece.waiting:
                copy.wait_recv()
            piece.consume()

    def run(pairs):
        for tick in range(len(pairs) + 7):
            for index, pair in enumerate(pairs):
                if 0 <= tick - index <= 7:
                    for piece in pair:
                        advance(piece, tick - index)

    def lanes(index, width):
        return pl.ds(pl.multiple_of(index * width, TILE), width)

    first, second = 2 * core, 2 * core + 1

    def basis_product(left, right):
        return transposed_product(basis_all[:, lanes(left, block)], basis_all[:, lanes(right, block)]) * weight

    def upper_tiles(value):
        middle = value.shape[0] // 2
        return pieces_to_tiles(value[:middle]) + pieces_to_tiles(value[middle:, middle:])

    def square_at(ref, offset, rows, cols):
        parts = [
            ref[pl.ds(offset + i * (rows // 8), rows // 8)].reshape(rows, TILE) for i in range(cols // TILE)
        ]
        return jnp.concatenate(parts, axis=1)

    def upper_at(ref, offset, size):
        middle = size // 2
        top = square_at(ref, offset, middle, size)
        corner = square_at(ref, offset + middle * size // 1024, middle, middle)
        return top, corner

    square = block * block // 1024

    def put_diagonal(owner, offset, index):
        top, corner = upper_at(basis_gram_tiles.at[owner], offset, block)
        middle = block // 2
        whole = jnp.concatenate([top, jnp.concatenate([top[:, middle:].T, corner], axis=1)], axis=0)
        unit = lax.broadcasted_iota(jnp.int32, whole.shape, 0) == lax.broadcasted_iota(jnp.int32, whole.shape, 1)
        window = slice(index * block, (index + 1) * block)
        operator[window, window] = jnp.where(unit, 1.0, 0.0) - whole

    def put_square(owner, offset, left, right):
        whole = -square_at(basis_gram_tiles.at[owner], offset, block, block)
        rows, cols = slice(left * block, (left + 1) * block), slice(right * block, (right + 1) * block)
        operator[rows, cols] = whole
        operator[cols, rows] = whole.T

    def consume_diagonals():
        offset = basis_gram[0].offset
        for owner in range(2):
            put_diagonal(owner, offset, 2 * owner)
            put_diagonal(owner, offset + square - square // 4, 2 * owner + 1)

    def consume_square(piece, pairs):
        for owner, (left, right) in enumerate(pairs):
            put_square(owner, piece.offset, left, right)

    def produce_coeffs(index):
        return pieces_to_tiles(
            transposed_product(basis_all[:, index * block : (index + 1) * block], block_half[...]) * weight
        )

    def consume_coeffs(index):
        piece = coeffs[index]
        value = square_at(coeffs_tiles, piece.offset, block, half)
        window = slice(index * block, (index + 1) * block)
        change = matrix_product(operator[:, window], value)
        removed = matrix_product(basis_all[:, window], value)
        if index == 0:
            correction[...] = change
            residual[core] = block_half[...] - removed
        else:
            correction[...] += change
            residual[core] -= removed

    for piece in basis_gram:
        piece.out, piece.shared = basis_gram_tiles.at[core], True
    for piece in coeffs:
        piece.out, piece.shared = coeffs_tiles, False
    for piece in gram:
        piece.out, piece.shared = gram_tiles.at[core], True
    basis_gram[0].produce = lambda: upper_tiles(basis_product(first, first)) + upper_tiles(
        basis_product(second, second)
    )
    basis_gram[1].produce = lambda: pieces_to_tiles(basis_product(first, second))
    basis_gram[2].produce = lambda: pieces_to_tiles(basis_product(second, lax.rem(second + 1, 4)))
    basis_gram[3].produce = lambda: pieces_to_tiles(basis_product(core, core + 2))
    basis_gram[0].consume = consume_diagonals
    basis_gram[1].consume = lambda: consume_square(basis_gram[1], ((0, 1), (2, 3)))
    basis_gram[2].consume = lambda: consume_square(basis_gram[2], ((1, 2), (3, 0)))
    basis_gram[3].consume = lambda: consume_square(basis_gram[3], ((0, 2), (1, 3)))
    for index, piece in enumerate(coeffs):
        piece.produce = functools.partial(produce_coeffs, index)
        piece.consume = functools.partial(consume_coeffs, index)

    for copy in shared:
        copy.wait_recv()
    run([basis_gram[0:2], basis_gram[3:1:-1], coeffs[0:2], coeffs[2:4]])

    residual[core] -= matrix_product(basis_all[...], correction[...])
    swap = start(residual.at[core], residual.at[core], extra_send.at[2], extra_recv.at[2], partner)

    def produce_cross():
        swap.wait_recv()
        left = residual[0, :, lanes(core, half // 2)]
        return pieces_to_tiles(transposed_product(left, residual[1]) * weight)

    def consume_corners():
        gram_ref[...] = jnp.zeros_like(gram_ref)
        for owner in range(2):
            top, corner = upper_at(gram_tiles.at[owner], gram[0].offset, half)
            middle, base = half // 2, owner * half
            gram_ref[base : base + middle, base : base + half] = top
            gram_ref[base + middle : base + half, base + middle : base + half] = corner

    def consume_cross():
        middle = half // 2
        for owner in range(2):
            gram_ref[owner * middle : (owner + 1) * middle, half:] = square_at(
                gram_tiles.at[owner], gram[1].offset, middle, half
            )

    gram[0].produce = lambda: upper_tiles(transposed_product(residual[core], residual[core]) * weight)
    gram[0].consume = consume_corners
    gram[1].produce = produce_cross
    gram[1].consume = consume_cross
    run([gram])
    for owner in range(2):
        residual_ref[:, owner * half : (owner + 1) * half] = residual[owner, mine, :]
    for copy in sent:
        copy.wait_send()


def orthogonalize(basis, block, counts):
    slots, columns = basis.shape
    width = block.shape[1]
    row_size, grp_size = lax.axis_size("row"), lax.axis_size("grp")
    across, down = plane_sides(row_size // 2)
    sizes = {"x": across, "y": down, "z": grp_size}
    plan = make_plan(columns, width, sizes)
    basis_gram, coeffs, gram, place = plan
    weight = 1.0 / (slots * row_size * grp_size)
    half = width // 2
    vmem = pl.BlockSpec(memory_space=pltpu.VMEM)

    def tiles(*shape):
        return pltpu.VMEM(shape + (8, TILE), jnp.float32)

    def total(group):
        return sum(piece.tiles for piece in group)

    return pl.pallas_call(
        functools.partial(orthogonalize_kernel, plan, sizes, weight),
        out_shape=(
            jax.ShapeDtypeStruct((slots, width), jnp.float32),
            jax.ShapeDtypeStruct((width, width), jnp.float32),
        ),
        in_specs=[pl.BlockSpec(memory_space=pltpu.SMEM), vmem, vmem],
        out_specs=(vmem, vmem),
        scratch_shapes=[
            pltpu.VMEM((2 * slots, columns), jnp.float32),
            pltpu.VMEM((2 * slots, half), jnp.float32),
            pltpu.VMEM((slots, half), jnp.float32),
            tiles(place["source"]),
            tiles(place["held"]),
            tiles(place["partial"]),
            tiles(2, total(basis_gram)),
            tiles(total(coeffs)),
            tiles(2, total(gram)),
            pltpu.VMEM((columns, columns), jnp.float32),
            pltpu.VMEM((columns, half), jnp.float32),
            pltpu.VMEM((2, 2 * slots, half), jnp.float32),
            pltpu.SemaphoreType.DMA((place["copy"],)),
            pltpu.SemaphoreType.DMA((place["copy"],)),
            pltpu.SemaphoreType.DMA((3,)),
            pltpu.SemaphoreType.DMA((3,)),
        ],
        compiler_params=pltpu.CompilerParams(collective_id=0, has_side_effects=True),
        name="orthogonalize",
    )(counts, basis, block)


def eliminate(block):
    size = block.shape[0]
    count = size // 8
    sub = lax.broadcasted_iota(jnp.int32, (8, size), 0)
    lane = lax.broadcasted_iota(jnp.int32, (8, size), 1)
    left = [block[8 * b : 8 * b + 8] for b in range(count)]
    right = [(lane == sub + 8 * b).astype(jnp.float32) for b in range(count)]
    for j in range(size):
        home, inner = divmod(j, 8)
        row = left[home][inner : inner + 1]
        companion = right[home][inner : inner + 1]
        inverse = 1.0 / row[:, j : j + 1]
        row = row * inverse
        companion = companion * inverse
        for b in range(home, count):
            if b == home and inner == 7:
                continue
            factor = jnp.broadcast_to(left[b][:, j : j + 1], (8, size))
            if b == home:
                factor = jnp.where(sub > inner, factor, 0.0)
            left[b] = left[b] - factor * row
            right[b] = right[b] - factor * companion
    upper, inverted = [], []
    for b in range(count):
        diagonal = jnp.sum(jnp.where(lane == sub + 8 * b, left[b], 0.0), axis=1, keepdims=True)
        root = 1.0 / jnp.sqrt(diagonal)
        upper.append(jnp.where(lane >= sub + 8 * b, left[b] * root, 0.0))
        inverted.append(jnp.where(lane <= sub + 8 * b, right[b] * root, 0.0))
    return jnp.concatenate(upper, axis=0), jnp.concatenate(inverted, axis=0)


def factor_kernel(gram_ref, residual_ref, new_ref, factor_ref, work, rest):
    size = gram_ref.shape[0]
    work[...] = gram_ref[...]
    rest[...] = residual_ref[...]

    def step(index, carry):
        window = pl.ds(pl.multiple_of(index * TILE, TILE), TILE)
        upper, inverted = eliminate(work[window, window])
        panel = matrix_product(inverted, work[window, :])
        column = lax.broadcasted_iota(jnp.int32, (TILE, size), 1)
        panel = jnp.where(column >= (index + 1) * TILE, panel, 0.0)
        factor_ref[window, :] = panel
        factor_ref[window, window] = upper
        work[...] -= transposed_product(panel, panel)
        solved = lax.dot_general(
            rest[:, window],
            inverted,
            (((1,), (1,)), ((), ())),
            precision=HIGHEST,
            preferred_element_type=jnp.float32,
        )
        new_ref[:, window] = solved
        rest[...] -= matrix_product(solved, panel)
        return carry

    lax.fori_loop(0, size // TILE, step, 0)


def factor_and_solve(gram, residual):
    vmem = pl.BlockSpec(memory_space=pltpu.VMEM)
    return pl.pallas_call(
        factor_kernel,
        out_shape=(
            jax.ShapeDtypeStruct(residual.shape, jnp.float32),
            jax.ShapeDtypeStruct(gram.shape, jnp.float32),
        ),
        in_specs=[vmem, vmem],
        out_specs=(vmem, vmem),
        scratch_shapes=[pltpu.VMEM(gram.shape, jnp.float32), pltpu.VMEM(residual.shape, jnp.float32)],
        name="factor_and_solve",
    )(gram, residual)


def body(basis, block, counts):
    residual, gram = orthogonalize(basis, block, counts)
    return factor_and_solve(gram, residual)


def solution(mesh):
    placed = (P(("grp", "row"), None), P(("grp", "row"), None), P("grp", "row"))
    return jax.shard_map(
        body, mesh=mesh, in_specs=placed, out_specs=(P(("grp", "row"), None), P()), check_vma=False
    )
```

time: 242 us -> 151 us (0.62); the launches traced: 239 us -> 151 us
  Pallas kernels: 220 us -> 150 us
  matrix products: 17.1 us -> 0 us
    pallas_call x3 -> x1, Pallas kernels: 168 us -> 96.8 us  [orthogonalize(): pl.pallas_call(functools.partial(orthogonalize_kernel, plan, sizes, weigh...]
    dot_general x5 -> x0, matrix products: 17.1 us -> none  [the longest x3 9.96 us: transposed_product(): lax.dot_general(left, right, (((0,), (0,)), ((), ())), precision=HIGHEST,...]
where the time goes in v1:
time: 151 us
  Pallas kernels  150 us (99%)
    pallas_call x1, Pallas kernels, orthogonalize(): pl.pallas_call(functools.partial(orthogonalize_kernel, plan, sizes, weigh...  96.8 us
    pallas_call x1, Pallas kernels, factor_and_solve(): pl.pallas_call(factor_kernel, out_shape=(jax.ShapeDtypeStruct(residual.sh...  52.8 us

profile of v1, /device:TPU:1, one launch (start us, length us, event | category | flops | bytes accessed | tf_op | source)
XLA Modules:
  0.0 150.8 jit_solution(7903029755570498397)
XLA Ops:
  1.3 96.8 %orthogonalize.1 = (f32[256,512]{1,0:T(8,128)}, f32[512,512]{1,0:T(8,128)}) custom-call(s32[1,1]{1,0:T(1,128)S(6)} %copy.5.counts_ref, f32[256,1024]{1,0:T(8,128)} %basis_ref.1, f32[256,512]{1,0:T(8,128)} %block_ref.1), custom_call_target="tpu_custom_call" | custom-call | tf_op jit(solution)/shard_map/orthogonalize/pallas_call | solution.py:406
  98.0 52.8 %factor_and_solve.1 = (f32[256,512]{1,0:T(8,128)}, f32[512,512]{1,0:T(8,128)}) custom-call(f32[512,512]{1,0:T(8,128)} %get-tuple-element.4.gram_ref, f32[256,512]{1,0:T(8,128)} %get-tuple-element.5.residual_ref), custom_call_target="tpu_custom_call" | custom-call | tf_op jit(solution)/shard_map/factor_and_solve/pallas_call | solution.py:498

commit v2 on v1

--- a/solution.py
+++ b/solution.py
@@ -434,63 +434,92 @@
     )(counts, basis, block)
 
 
-def eliminate(block):
-    size = block.shape[0]
-    count = size // 8
-    sub = lax.broadcasted_iota(jnp.int32, (8, size), 0)
-    lane = lax.broadcasted_iota(jnp.int32, (8, size), 1)
-    left = [block[8 * b : 8 * b + 8] for b in range(count)]
-    right = [(lane == sub + 8 * b).astype(jnp.float32) for b in range(count)]
-    for j in range(size):
-        home, inner = divmod(j, 8)
-        row = left[home][inner : inner + 1]
-        companion = right[home][inner : inner + 1]
-        inverse = 1.0 / row[:, j : j + 1]
-        row = row * inverse
-        companion = companion * inverse
-        for b in range(home, count):
-            if b == home and inner == 7:
-                continue
-            factor = jnp.broadcast_to(left[b][:, j : j + 1], (8, size))
-            if b == home:
-                factor = jnp.where(sub > inner, factor, 0.0)
-            left[b] = left[b] - factor * row
-            right[b] = right[b] - factor * companion
+BLOCK = 64
+GROUP = 8
+
+
+def eliminate(square):
+    size = square.shape[0]
+    count = size // GROUP
+    shape = (GROUP, 2 * size)
+    sub = lax.broadcasted_iota(jnp.int32, shape, 0)
+    lane = lax.broadcasted_iota(jnp.int32, shape, 1)
+    wide = [
+        jnp.concatenate(
+            [
+                square[GROUP * b : GROUP * (b + 1)],
+                (lane[:, :size] == sub[:, :size] + GROUP * b).astype(jnp.float32),
+            ],
+            axis=1,
+        )
+        for b in range(count)
+    ]
+
+    def across(value, index):
+        return jnp.broadcast_to(value[:, index : index + 1], shape)
+
+    def down(value, index):
+        return jnp.broadcast_to(value[index : index + 1], shape)
+
+    roots = []
+    for g in range(count):
+        columns = {b: [across(wide[b], GROUP * g + i) for i in range(GROUP)] for b in range(g, count)}
+        root = jnp.zeros(shape, jnp.float32)
+        for i in range(GROUP):
+            pivot = down(columns[g][i], i)
+            inverse = 1.0 / pivot
+            root = jnp.where(sub == i, 1.0 / jnp.sqrt(pivot), root)
+            later = [down(columns[g][j], i) for j in range(i + 1, GROUP)]
+            row = down(wide[g], i)
+            for b in range(g, count):
+                factor = columns[b][i] * inverse
+                if b == g:
+                    if i == GROUP - 1:
+                        continue
+                    factor = jnp.where(sub > i, factor, 0.0)
+                for j in range(i + 1, GROUP):
+                    columns[b][j] = columns[b][j] - factor * later[j - i - 1]
+                wide[b] = wide[b] - factor * row
+        roots.append(root)
     upper, inverted = [], []
     for b in range(count):
-        diagonal = jnp.sum(jnp.where(lane == sub + 8 * b, left[b], 0.0), axis=1, keepdims=True)
-        root = 1.0 / jnp.sqrt(diagonal)
-        upper.append(jnp.where(lane >= sub + 8 * b, left[b] * root, 0.0))
-        inverted.append(jnp.where(lane <= sub + 8 * b, right[b] * root, 0.0))
+        value = wide[b] * roots[b]
+        upper.append(jnp.where((lane >= sub + GROUP * b)[:, :size], value[:, :size], 0.0))
+        inverted.append(jnp.where((lane <= sub + GROUP * b)[:, :size], value[:, size:], 0.0))
     return jnp.concatenate(upper, axis=0), jnp.concatenate(inverted, axis=0)
 
 
 def factor_kernel(gram_ref, residual_ref, new_ref, factor_ref, work, rest):
     size = gram_ref.shape[0]
+    steps = size // BLOCK
     work[...] = gram_ref[...]
     rest[...] = residual_ref[...]
-
-    def step(index, carry):
-        window = pl.ds(pl.multiple_of(index * TILE, TILE), TILE)
-        upper, inverted = eliminate(work[window, window])
-        panel = matrix_product(inverted, work[window, :])
-        column = lax.broadcasted_iota(jnp.int32, (TILE, size), 1)
-        panel = jnp.where(column >= (index + 1) * TILE, panel, 0.0)
-        factor_ref[window, :] = panel
-        factor_ref[window, window] = upper
-        work[...] -= transposed_product(panel, panel)
+    square = work[:BLOCK, :BLOCK]
+    for step in range(steps):
+        here, after, beyond = (BLOCK * (step + i) for i in range(3))
+        upper, inverted = eliminate(square)
+        if step:
+            factor_ref[here:after, :here] = jnp.zeros((BLOCK, here), jnp.float32)
+        factor_ref[here:after, here:after] = upper
+        if after < size:
+            near = matrix_product(inverted, work[here:after, after:beyond])
+            square = work[after:beyond, after:beyond] - transposed_product(near, near)
+            factor_ref[here:after, after:beyond] = near
+            if beyond < size:
+                panel = matrix_product(inverted, work[here:after, beyond:])
+                factor_ref[here:after, beyond:] = panel
+                work[after:beyond, beyond:] -= transposed_product(near, panel)
+                work[beyond:, beyond:] -= transposed_product(panel, panel)
         solved = lax.dot_general(
-            rest[:, window],
+            rest[:, here:after],
             inverted,
             (((1,), (1,)), ((), ())),
             precision=HIGHEST,
             preferred_element_type=jnp.float32,
         )
-        new_ref[:, window] = solved
-        rest[...] -= matrix_product(solved, panel)
-        return carry
-
-    lax.fori_loop(0, size // TILE, step, 0)
+        new_ref[:, here:after] = solved
+        if after < size:
+            rest[:, after:] -= matrix_product(solved, factor_ref[here:after, after:])
 
 
 def factor_and_solve(gram, residual):

time: 151 us -> 122 us (0.81)
  Pallas kernels: 150 us -> 120 us
    pallas_call x1, Pallas kernels: 52.8 us -> 23.3 us  [factor_and_solve(): pl.pallas_call(factor_kernel, out_shape=(jax.ShapeDtypeStruct(residual.sh...]
where the time goes in v2:
time: 122 us; the launch traced here: 121 us
  Pallas kernels  120 us (98%)
  between operations  1.28 us (1%)
    pallas_call x1, Pallas kernels, orthogonalize(): pl.pallas_call(functools.partial(orthogonalize_kernel, plan, sizes, weigh...  96.8 us
    pallas_call x1, Pallas kernels, factor_and_solve(): pl.pallas_call(factor_kernel, out_shape=(jax.ShapeDtypeStruct(residual.sh...  23.3 us

profile of v2, /device:TPU:1, one launch (start us, length us, event | category | flops | bytes accessed | tf_op | source)
XLA Modules:
  0.0 121.4 jit_solution(9222464178104137521)
XLA Ops:
  1.3 96.8 %orthogonalize.1 = (f32[256,512]{1,0:T(8,128)}, f32[512,512]{1,0:T(8,128)}) custom-call(s32[1,1]{1,0:T(1,128)S(6)} %copy.5.counts_ref, f32[256,1024]{1,0:T(8,128)} %basis_ref.1, f32[256,512]{1,0:T(8,128)} %block_ref.1), custom_call_target="tpu_custom_call" | custom-call | tf_op jit(solution)/shard_map/orthogonalize/pallas_call | solution.py:406
  98.0 23.3 %factor_and_solve.1 = (f32[256,512]{1,0:T(8,128)}, f32[512,512]{1,0:T(8,128)}) custom-call(f32[512,512]{1,0:T(8,128)} %get-tuple-element.4.gram_ref, f32[256,512]{1,0:T(8,128)} %get-tuple-element.5.residual_ref), custom_call_target="tpu_custom_call" | custom-call | tf_op jit(solution)/shard_map/factor_and_solve/pallas_call | solution.py:527

commit v3 on v2

--- a/solution.py
+++ b/solution.py
@@ -27,6 +27,13 @@
     return jnp.dot(left, right, precision=HIGHEST, preferred_element_type=jnp.float32)
 
 
+AXES = {"x": "x", "y": "y", "z": "z", "n": "near", "f": "far", "p": "plane"}
+FIRST_ROUTES = ("xyz", "yxz", "zxy", "yxz", "xyz", "yxz", "yxz", "xyz")
+FIRST_ORDER = (0, 1, 2, 3, 1, 0, 4, 5, 3, 2, 1, 0, 6, 7, 5, 4, 3, 2, 1, 0, 7, 6, 5, 4, 3, 2, 1, 0, 7, 6, 5, 4, 3, 2, 1, 0, 7, 6, 5, 4, 3, 2, 1, 0, 7, 6, 5, 4, 3, 2, 1, 0, -1, -2, 7, 6, 5, 4, 3, 2, -3, -4, -5, -6, 7, 6, -7, -8)
+SECOND_ROUTES = ("pz", "zp")
+SECOND_ORDER = (0, 1, 0, 1, 0, 1, 1, 0, 0, 1, 0, -1, 1, -2)
+
+
 def plane_sides(chips):
     side = math.isqrt(chips)
     while chips % side:
@@ -39,23 +46,20 @@
         self.used = tiles
         self.tiles = -(-tiles // chips) * chips
         self.order = order
+        self.step = 0
 
 
 def make_plan(basis_columns, block_columns, sizes):
-    chips = sizes["x"] * sizes["y"] * sizes["z"]
+    chips = sizes["plane"] * sizes["z"]
     block = basis_columns // 4
     half = block_columns // 2
     square = block * block // 1024
     corner = half * half // 1024
-    forward, backward = ("x", "y", "z"), ("y", "x", "z")
-    basis_gram = [
-        Piece(2 * (square - square // 4), forward, chips),
-        Piece(square, backward, chips),
-        Piece(square, backward, chips),
-        Piece(square, forward, chips),
-    ]
-    coeffs = [Piece(block * half // 1024, (forward, backward)[i % 2], chips) for i in range(4)]
-    gram = [Piece(corner - corner // 4, forward, chips), Piece(corner // 2, backward, chips)]
+    diagonal, corner = square - square // 4, corner - corner // 4
+    shapes = [2 * diagonal, square, square, square] + [block * half // 1024] * 4
+    first = [Piece(tiles, [AXES[letter] for letter in route], chips) for tiles, route in zip(shapes, FIRST_ROUTES)]
+    second = [Piece(tiles, [AXES[letter] for letter in route], chips) for tiles, route in zip((corner, half * half // 2048), SECOND_ROUTES)]
+    basis_gram, coeffs, gram = first[:4], first[4:], second
     place = dict(copy=0, source=0, held=0, partial=0)
     for group in (basis_gram, coeffs, gram):
         offset = 0
@@ -121,19 +125,32 @@
     row = lax.axis_index("row")
     core = lax.rem(row, 2)
     chip = lax.div(row, 2)
-    me = {"x": lax.rem(chip, sizes["x"]), "y": lax.div(chip, sizes["x"]), "z": lax.axis_index("grp")}
+    me = {
+        "x": lax.rem(chip, sizes["x"]),
+        "y": lax.div(chip, sizes["x"]),
+        "z": lax.axis_index("grp"),
+        "plane": chip,
+        "near": lax.rem(lax.axis_index("grp"), sizes["near"]),
+        "far": lax.div(lax.axis_index("grp"), sizes["near"]),
+    }
     partner = {"row": row + 1 - 2 * core}
 
     def peer(axis, k):
         other = lax.rem(me[axis] + k, sizes[axis])
         if axis == "z":
             return {"grp": other}
+        if axis == "near":
+            return {"grp": me["far"] * sizes["near"] + other}
+        if axis == "far":
+            return {"grp": other * sizes["near"] + me["near"]}
+        if axis == "plane":
+            return {"row": other * 2 + core}
         x, y = (other, me["y"]) if axis == "x" else (me["x"], other)
         return {"row": (y * sizes["x"] + x) * 2 + core}
 
     barrier = pltpu.get_barrier_semaphore()
     pl.semaphore_signal(barrier, inc=1, device_id=partner, device_id_type=MESH)
-    for axis in sizes:
+    for axis in ("plane", "z"):
         for k in range(1, sizes[axis]):
             pl.semaphore_signal(barrier, inc=1, device_id=peer(axis, k), device_id_type=MESH)
     sent = []
@@ -158,7 +175,7 @@
     basis_all[mine, :] = jnp.where(live, basis_ref[...], 0.0)
     block_send[...] = jnp.where(live, block_ref[:, far], 0.0)
     block_half[mine, :] = jnp.where(live, block_ref[:, near], 0.0)
-    pl.semaphore_wait(barrier, 1 + sum(size - 1 for size in sizes.values()))
+    pl.semaphore_wait(barrier, sizes["plane"] + sizes["z"] - 1)
     shared = [
         start(basis_all.at[mine], basis_all.at[mine], extra_send.at[0], extra_recv.at[0], partner),
         start(block_send, block_half.at[mine], extra_send.at[1], extra_recv.at[1], partner),
@@ -214,50 +231,50 @@
             index = stage["gather"] + k - 1
             piece.waiting.append(start(place, place, send_sem.at[index], recv_sem.at[index], peer(axis, k)))
 
-    def advance(piece, step):
+    def stage_source(piece):
+        offset = piece.source
+        for value in piece.produce():
+            source[pl.ds(offset, value.shape[0])] = value
+            offset += value.shape[0]
+        if piece.used < piece.tiles:
+            source[pl.ds(offset, piece.tiles - piece.used)] = jnp.zeros(
+                (piece.tiles - piece.used, 8, TILE), jnp.float32
+            )
+
+    def advance(piece):
+        depth = len(piece.stages)
+        step = piece.step
+        piece.step += 1
         if step == 0:
-            blocks = piece.produce()
-            offset = piece.source
-            for value in blocks:
-                source[pl.ds(offset, value.shape[0])] = value
-                offset += value.shape[0]
-            if piece.used < piece.tiles:
-                source[pl.ds(offset, piece.tiles - piece.used)] = jnp.zeros(
-                    (piece.tiles - piece.used, 8, TILE), jnp.float32
-                )
+            stage_source(piece)
             scatter(piece, 0)
-        elif step < 3:
+            return
+        if step < depth:
             stage = piece.stages[step - 1]
             partial[pl.ds(stage["partial"], stage["size"])] = reduced(piece, step - 1)
             scatter(piece, step)
-        elif step == 3:
-            size = piece.stages[2]["size"]
-            piece.out[pl.ds(piece.offset + position(piece, 3), size)] = reduced(piece, 2)
-            gather(piece, 2)
-        elif step < 6:
-            for copy in piece.waiting:
-                copy.wait_recv()
-            gather(piece, 5 - step)
-        elif step == 6:
-            for copy in piece.waiting:
-                copy.wait_recv()
-            if piece.shared:
-                place = piece.out.at[pl.ds(piece.offset, piece.tiles)]
-                index = piece.partner
-                piece.waiting = [start(place, place, send_sem.at[index], recv_sem.at[index], partner)]
+            return
+        if step == depth:
+            size = piece.stages[-1]["size"]
+            piece.out[pl.ds(piece.offset + position(piece, depth), size)] = reduced(piece, depth - 1)
+            gather(piece, depth - 1)
+            return
+        for copy in piece.waiting:
+            copy.wait_recv()
+        piece.waiting = []
+        if step < 2 * depth:
+            gather(piece, 2 * depth - 1 - step)
+        elif step == 2 * depth and piece.shared:
+            place = piece.out.at[pl.ds(piece.offset, piece.tiles)]
+            index = piece.partner
+            piece.waiting = [start(place, place, send_sem.at[index], recv_sem.at[index], partner)]
+
+    def run(pieces, order):
+        for entry in order:
+            if entry < 0:
+                pieces[~entry].consume()
             else:
-                piece.consume()
-        elif step == 7 and piece.shared:
-            for copy in piece.waiting:
-                copy.wait_recv()
-            piece.consume()
-
-    def run(pairs):
-        for tick in range(len(pairs) + 7):
-            for index, pair in enumerate(pairs):
-                if 0 <= tick - index <= 7:
-                    for piece in pair:
-                        advance(piece, tick - index)
+                advance(pieces[entry])
 
     def lanes(index, width):
         return pl.ds(pl.multiple_of(index * width, TILE), width)
@@ -349,10 +366,12 @@
 
     for copy in shared:
         copy.wait_recv()
-    run([basis_gram[0:2], basis_gram[3:1:-1], coeffs[0:2], coeffs[2:4]])
+    run(basis_gram + coeffs, FIRST_ORDER)
 
     residual[core] -= matrix_product(basis_all[...], correction[...])
     swap = start(residual.at[core], residual.at[core], extra_send.at[2], extra_recv.at[2], partner)
+
+    gram_ref[...] = jnp.zeros_like(gram_ref)
 
     def produce_cross():
         swap.wait_recv()
@@ -360,7 +379,6 @@
         return pieces_to_tiles(transposed_product(left, residual[1]) * weight)
 
     def consume_corners():
-        gram_ref[...] = jnp.zeros_like(gram_ref)
         for owner in range(2):
             top, corner = upper_at(gram_tiles.at[owner], gram[0].offset, half)
             middle, base = half // 2, owner * half
@@ -378,7 +396,7 @@
     gram[0].consume = consume_corners
     gram[1].produce = produce_cross
     gram[1].consume = consume_cross
-    run([gram])
+    run(gram, SECOND_ORDER)
     for owner in range(2):
         residual_ref[:, owner * half : (owner + 1) * half] = residual[owner, mine, :]
     for copy in sent:
@@ -390,7 +408,8 @@
     width = block.shape[1]
     row_size, grp_size = lax.axis_size("row"), lax.axis_size("grp")
     across, down = plane_sides(row_size // 2)
-    sizes = {"x": across, "y": down, "z": grp_size}
+    near = 2 - grp_size % 2
+    sizes = {"x": across, "y": down, "z": grp_size, "plane": across * down, "near": near, "far": grp_size // near}
     plan = make_plan(columns, width, sizes)
     basis_gram, coeffs, gram, place = plan
     weight = 1.0 / (slots * row_size * grp_size)

time: 122 us -> 110 us (0.902)
  Pallas kernels: 120 us -> 108 us
    pallas_call x1, Pallas kernels: 96.8 us -> 84.8 us  [orthogonalize(): pl.pallas_call(functools.partial(orthogonalize_kernel, plan, sizes, weigh...]
where the time goes in v3:
time: 110 us; the launch traced here: 109 us
  Pallas kernels  108 us (98%)
  between operations  1.28 us (1%)
    pallas_call x1, Pallas kernels, orthogonalize(): pl.pallas_call(functools.partial(orthogonalize_kernel, plan, sizes, weigh...  84.8 us
    pallas_call x1, Pallas kernels, factor_and_solve(): pl.pallas_call(factor_kernel, out_shape=(jax.ShapeDtypeStruct(residual.sh...  23.4 us

profile of v3, /device:TPU:1, one launch (start us, length us, event | category | flops | bytes accessed | tf_op | source)
XLA Modules:
  0.0 109.4 jit_solution(8574641081296593565)
XLA Ops:
  1.3 84.8 %orthogonalize.1 = (f32[256,512]{1,0:T(8,128)}, f32[512,512]{1,0:T(8,128)}) custom-call(s32[1,1]{1,0:T(1,128)S(6)} %copy.5.counts_ref, f32[256,1024]{1,0:T(8,128)} %basis_ref.1, f32[256,512]{1,0:T(8,128)} %block_ref.1), custom_call_target="tpu_custom_call" | custom-call | tf_op jit(solution)/shard_map/orthogonalize/pallas_call | solution.py:425
  86.1 23.4 %factor_and_solve.1 = (f32[256,512]{1,0:T(8,128)}, f32[512,512]{1,0:T(8,128)}) custom-call(f32[512,512]{1,0:T(8,128)} %get-tuple-element.4.gram_ref, f32[256,512]{1,0:T(8,128)} %get-tuple-element.5.residual_ref), custom_call_target="tpu_custom_call" | custom-call | tf_op jit(solution)/shard_map/factor_and_solve/pallas_call | solution.py:546

commit v4 on v3

--- a/solution.py
+++ b/solution.py
@@ -95,10 +95,13 @@
     sizes,
     weight,
     counts_ref,
+    basis_hbm,
+    block_hbm,
+    residual_ref,
+    gram_ref,
     basis_ref,
     block_ref,
-    residual_ref,
-    gram_ref,
+    load_sem,
     basis_all,
     block_half,
     block_send,
@@ -122,6 +125,12 @@
     half = block_ref.shape[1] // 2
     block = columns // 4
 
+    loads = [
+        pltpu.make_async_copy(basis_hbm, basis_ref, load_sem.at[0]),
+        pltpu.make_async_copy(block_hbm, block_ref, load_sem.at[1]),
+    ]
+    for copy in loads:
+        copy.start()
     row = lax.axis_index("row")
     core = lax.rem(row, 2)
     chip = lax.div(row, 2)
@@ -172,6 +181,8 @@
     mine = pl.ds(pl.multiple_of(core * slots, 8), slots)
     near = pl.ds(pl.multiple_of(core * half, TILE), half)
     far = pl.ds(pl.multiple_of((1 - core) * half, TILE), half)
+    for copy in loads:
+        copy.wait()
     basis_all[mine, :] = jnp.where(live, basis_ref[...], 0.0)
     block_send[...] = jnp.where(live, block_ref[:, far], 0.0)
     block_half[mine, :] = jnp.where(live, block_ref[:, near], 0.0)
@@ -428,9 +439,12 @@
             jax.ShapeDtypeStruct((slots, width), jnp.float32),
             jax.ShapeDtypeStruct((width, width), jnp.float32),
         ),
-        in_specs=[pl.BlockSpec(memory_space=pltpu.SMEM), vmem, vmem],
+        in_specs=[pl.BlockSpec(memory_space=pltpu.SMEM)] + [pl.BlockSpec(memory_space=pl.ANY)] * 2,
         out_specs=(vmem, vmem),
         scratch_shapes=[
+            pltpu.VMEM((slots, columns), jnp.float32),
+            pltpu.VMEM((slots, width), jnp.float32),
+            pltpu.SemaphoreType.DMA((2,)),
             pltpu.VMEM((2 * slots, columns), jnp.float32),
             pltpu.VMEM((2 * slots, half), jnp.float32),
             pltpu.VMEM((slots, half), jnp.float32),
@@ -457,6 +471,10 @@
 GROUP = 8
 
 
+BLOCK = 64
+GROUP = 8
+
+
 def eliminate(square):
     size = square.shape[0]
     count = size // GROUP
@@ -483,23 +501,23 @@
     roots = []
     for g in range(count):
         columns = {b: [across(wide[b], GROUP * g + i) for i in range(GROUP)] for b in range(g, count)}
-        root = jnp.zeros(shape, jnp.float32)
+        columns[g] = [jnp.where(lane < 2 * size, column, 0.0) for column in columns[g]]
+        pivots = jnp.ones(shape, jnp.float32)
         for i in range(GROUP):
             pivot = down(columns[g][i], i)
             inverse = 1.0 / pivot
-            root = jnp.where(sub == i, 1.0 / jnp.sqrt(pivot), root)
+            pivots = jnp.where(sub == i, pivot, pivots)
             later = [down(columns[g][j], i) for j in range(i + 1, GROUP)]
             row = down(wide[g], i)
             for b in range(g, count):
-                factor = columns[b][i] * inverse
-                if b == g:
-                    if i == GROUP - 1:
-                        continue
-                    factor = jnp.where(sub > i, factor, 0.0)
+                if b == g and i == GROUP - 1:
+                    continue
+                column = jnp.where(sub > i, columns[b][i], 0.0) if b == g else columns[b][i]
+                factor = column * inverse
                 for j in range(i + 1, GROUP):
                     columns[b][j] = columns[b][j] - factor * later[j - i - 1]
                 wide[b] = wide[b] - factor * row
-        roots.append(root)
+        roots.append(lax.rsqrt(pivots))
     upper, inverted = [], []
     for b in range(count):
         value = wide[b] * roots[b]
@@ -528,7 +546,11 @@
                 panel = matrix_product(inverted, work[here:after, beyond:])
                 factor_ref[here:after, beyond:] = panel
                 work[after:beyond, beyond:] -= transposed_product(near, panel)
-                work[beyond:, beyond:] -= transposed_product(panel, panel)
+                for start in range(beyond, size, 2 * BLOCK):
+                    stop = min(start + 2 * BLOCK, size)
+                    work[start:stop, start:] -= transposed_product(
+                        panel[:, start - beyond : stop - beyond], panel[:, start - beyond :]
+                    )
         solved = lax.dot_general(
             rest[:, here:after],
             inverted,

time: 110 us -> 105 us (0.955)
  Pallas kernels: 108 us -> 103 us
    pallas_call x1, Pallas kernels: 23.4 us -> 19.9 us  [factor_and_solve(): pl.pallas_call(factor_kernel, out_shape=(jax.ShapeDtypeStruct(residual.sh...]
    pallas_call x1, Pallas kernels: 84.8 us -> 83.5 us  [orthogonalize(): pl.pallas_call(functools.partial(orthogonalize_kernel, plan, sizes, weigh...]
where the time goes in v4:
time: 105 us
  Pallas kernels  103 us (98%)
  between operations  1.28 us (1%)
    pallas_call x1, Pallas kernels, orthogonalize(): pl.pallas_call(functools.partial(orthogonalize_kernel, plan, sizes, weigh...  83.5 us
    pallas_call x1, Pallas kernels, factor_and_solve(): pl.pallas_call(factor_kernel, out_shape=(jax.ShapeDtypeStruct(residual.sh...  19.9 us

profile of v4, /device:TPU:1, one launch (start us, length us, event | category | flops | bytes accessed | tf_op | source)
XLA Modules:
  0.0 104.7 jit_solution(3117407109433695482)
XLA Ops:
  1.3 83.5 %orthogonalize.1 = (f32[256,512]{1,0:T(8,128)}, f32[512,512]{1,0:T(8,128)}) custom-call(s32[1,1]{1,0:T(1,128)S(6)} %copy.5.counts_ref, f32[256,1024]{1,0:T(8,128)} %basis_hbm.1, f32[256,512]{1,0:T(8,128)} %block_hbm.1), custom_call_target="tpu_custom_call" | custom-call | tf_op jit(solution)/shard_map/orthogonalize/pallas_call | solution.py:436
  84.8 19.9 %factor_and_solve.1 = (f32[256,512]{1,0:T(8,128)}, f32[512,512]{1,0:T(8,128)}) custom-call(f32[512,512]{1,0:T(8,128)} %get-tuple-element.4.gram_ref, f32[256,512]{1,0:T(8,128)} %get-tuple-element.5.residual_ref), custom_call_target="tpu_custom_call" | custom-call | tf_op jit(solution)/shard_map/factor_and_solve/pallas_call | solution.py:568

commit v5 on v4

--- a/solution.py
+++ b/solution.py
@@ -97,11 +97,12 @@
     counts_ref,
     basis_hbm,
     block_hbm,
-    residual_ref,
+    residual_hbm,
     gram_ref,
     basis_ref,
     block_ref,
     load_sem,
+    store_sem,
     basis_all,
     block_half,
     block_send,
@@ -187,10 +188,12 @@
     block_send[...] = jnp.where(live, block_ref[:, far], 0.0)
     block_half[mine, :] = jnp.where(live, block_ref[:, near], 0.0)
     pl.semaphore_wait(barrier, sizes["plane"] + sizes["z"] - 1)
-    shared = [
-        start(basis_all.at[mine], basis_all.at[mine], extra_send.at[0], extra_recv.at[0], partner),
-        start(block_send, block_half.at[mine], extra_send.at[1], extra_recv.at[1], partner),
-    ]
+    wide = columns // 2
+    shared = []
+    for index, side in enumerate((1 - core, core)):
+        place = basis_all.at[mine, pl.ds(pl.multiple_of(side * wide, TILE), wide)]
+        shared.append(start(place, place, extra_send.at[index], extra_recv.at[index], partner))
+    shared.append(start(block_send, block_half.at[mine], extra_send.at[3], extra_recv.at[3], partner))
 
     def position(piece, depth):
         offset = 0
@@ -361,11 +364,18 @@
         piece.out, piece.shared = coeffs_tiles, False
     for piece in gram:
         piece.out, piece.shared = gram_tiles.at[core], True
-    basis_gram[0].produce = lambda: upper_tiles(basis_product(first, first)) + upper_tiles(
-        basis_product(second, second)
-    )
+    def produce_diagonals():
+        shared[0].wait_recv()
+        return upper_tiles(basis_product(first, first)) + upper_tiles(basis_product(second, second))
+
+    def produce_beyond():
+        shared[1].wait_recv()
+        shared[2].wait_recv()
+        return pieces_to_tiles(basis_product(second, lax.rem(second + 1, 4)))
+
+    basis_gram[0].produce = produce_diagonals
     basis_gram[1].produce = lambda: pieces_to_tiles(basis_product(first, second))
-    basis_gram[2].produce = lambda: pieces_to_tiles(basis_product(second, lax.rem(second + 1, 4)))
+    basis_gram[2].produce = produce_beyond
     basis_gram[3].produce = lambda: pieces_to_tiles(basis_product(core, core + 2))
     basis_gram[0].consume = consume_diagonals
     basis_gram[1].consume = lambda: consume_square(basis_gram[1], ((0, 1), (2, 3)))
@@ -375,17 +385,25 @@
         piece.produce = functools.partial(produce_coeffs, index)
         piece.consume = functools.partial(consume_coeffs, index)
 
-    for copy in shared:
-        copy.wait_recv()
     run(basis_gram + coeffs, FIRST_ORDER)
 
     residual[core] -= matrix_product(basis_all[...], correction[...])
+    stores = [
+        pltpu.make_async_copy(
+            residual.at[owner, mine],
+            residual_hbm.at[:, owner * half : (owner + 1) * half],
+            store_sem.at[owner],
+        )
+        for owner in range(2)
+    ]
     swap = start(residual.at[core], residual.at[core], extra_send.at[2], extra_recv.at[2], partner)
 
     gram_ref[...] = jnp.zeros_like(gram_ref)
 
     def produce_cross():
         swap.wait_recv()
+        for copy in stores:
+            copy.start()
         left = residual[0, :, lanes(core, half // 2)]
         return pieces_to_tiles(transposed_product(left, residual[1]) * weight)
 
@@ -408,8 +426,8 @@
     gram[1].produce = produce_cross
     gram[1].consume = consume_cross
     run(gram, SECOND_ORDER)
-    for owner in range(2):
-        residual_ref[:, owner * half : (owner + 1) * half] = residual[owner, mine, :]
+    for copy in stores:
+        copy.wait()
     for copy in sent:
         copy.wait_send()
 
@@ -440,10 +458,11 @@
             jax.ShapeDtypeStruct((width, width), jnp.float32),
         ),
         in_specs=[pl.BlockSpec(memory_space=pltpu.SMEM)] + [pl.BlockSpec(memory_space=pl.ANY)] * 2,
-        out_specs=(vmem, vmem),
+        out_specs=(pl.BlockSpec(memory_space=pl.ANY), vmem),
         scratch_shapes=[
             pltpu.VMEM((slots, columns), jnp.float32),
             pltpu.VMEM((slots, width), jnp.float32),
+            pltpu.SemaphoreType.DMA((2,)),
             pltpu.SemaphoreType.DMA((2,)),
             pltpu.VMEM((2 * slots, columns), jnp.float32),
             pltpu.VMEM((2 * slots, half), jnp.float32),
@@ -459,16 +478,12 @@
             pltpu.VMEM((2, 2 * slots, half), jnp.float32),
             pltpu.SemaphoreType.DMA((place["copy"],)),
             pltpu.SemaphoreType.DMA((place["copy"],)),
-            pltpu.SemaphoreType.DMA((3,)),
-            pltpu.SemaphoreType.DMA((3,)),
+            pltpu.SemaphoreType.DMA((4,)),
+            pltpu.SemaphoreType.DMA((4,)),
         ],
         compiler_params=pltpu.CompilerParams(collective_id=0, has_side_effects=True),
         name="orthogonalize",
     )(counts, basis, block)
-
-
-BLOCK = 64
-GROUP = 8
 
 
 BLOCK = 64
@@ -499,9 +514,16 @@
         return jnp.broadcast_to(value[index : index + 1], shape)
 
     roots = []
+
+    def shown(value):
+        return jnp.where(lane < 2 * size, value, 0.0)
+
+    home = [shown(across(wide[0], i)) for i in range(GROUP)]
     for g in range(count):
-        columns = {b: [across(wide[b], GROUP * g + i) for i in range(GROUP)] for b in range(g, count)}
-        columns[g] = [jnp.where(lane < 2 * size, column, 0.0) for column in columns[g]]
+        columns = {b: [across(wide[b], GROUP * g + i) for i in range(GROUP)] for b in range(g + 1, count)}
+        columns[g] = home
+        if g + 1 < count:
+            ahead = {b: [shown(across(wide[b], GROUP * (g + 1) + i)) for i in range(GROUP)] for b in (g, g + 1)}
         pivots = jnp.ones(shape, jnp.float32)
         for i in range(GROUP):
             pivot = down(columns[g][i], i)
@@ -509,6 +531,8 @@
             pivots = jnp.where(sub == i, pivot, pivots)
             later = [down(columns[g][j], i) for j in range(i + 1, GROUP)]
             row = down(wide[g], i)
+            if g + 1 < count:
+                cross = [down(value, i) for value in ahead[g]]
             for b in range(g, count):
                 if b == g and i == GROUP - 1:
                     continue
@@ -517,6 +541,10 @@
                 for j in range(i + 1, GROUP):
                     columns[b][j] = columns[b][j] - factor * later[j - i - 1]
                 wide[b] = wide[b] - factor * row
+                if g + 1 < count and b <= g + 1:
+                    ahead[b] = [value - factor * over for value, over in zip(ahead[b], cross)]
+        if g + 1 < count:
+            home = ahead[g + 1]
         roots.append(lax.rsqrt(pivots))
     upper, inverted = [], []
     for b in range(count):
@@ -526,15 +554,31 @@
     return jnp.concatenate(upper, axis=0), jnp.concatenate(inverted, axis=0)
 
 
-def factor_kernel(gram_ref, residual_ref, new_ref, factor_ref, work, rest):
-    size = gram_ref.shape[0]
+def factor_kernel(gram_hbm, residual_hbm, new_hbm, factor_hbm, work, rest, new_ref, factor_ref, load_sem, store_sem):
+    size = gram_hbm.shape[0]
     steps = size // BLOCK
-    work[...] = gram_ref[...]
-    rest[...] = residual_ref[...]
+    loads = [
+        pltpu.make_async_copy(gram_hbm.at[:BLOCK], work.at[:BLOCK], load_sem.at[0]),
+        pltpu.make_async_copy(gram_hbm.at[BLOCK:], work.at[BLOCK:], load_sem.at[1]),
+        pltpu.make_async_copy(residual_hbm, rest, load_sem.at[2]),
+    ]
+    for copy in loads:
+        copy.start()
+    stores = []
+
+    def store(source, target):
+        copy = pltpu.make_async_copy(source, target, store_sem.at[len(stores)])
+        copy.start()
+        stores.append(copy)
+
+    loads[0].wait()
     square = work[:BLOCK, :BLOCK]
     for step in range(steps):
         here, after, beyond = (BLOCK * (step + i) for i in range(3))
         upper, inverted = eliminate(square)
+        if step == 0:
+            loads[1].wait()
+            loads[2].wait()
         if step:
             factor_ref[here:after, :here] = jnp.zeros((BLOCK, here), jnp.float32)
         factor_ref[here:after, here:after] = upper
@@ -559,21 +603,34 @@
             preferred_element_type=jnp.float32,
         )
         new_ref[:, here:after] = solved
+        store(factor_ref.at[here:after], factor_hbm.at[here:after])
+        if after % TILE == 0:
+            store(new_ref.at[:, after - TILE : after], new_hbm.at[:, after - TILE : after])
         if after < size:
             rest[:, after:] -= matrix_product(solved, factor_ref[here:after, after:])
+    for copy in stores:
+        copy.wait()
 
 
 def factor_and_solve(gram, residual):
-    vmem = pl.BlockSpec(memory_space=pltpu.VMEM)
+    hbm = pl.BlockSpec(memory_space=pl.ANY)
+    copies = gram.shape[0] // BLOCK + gram.shape[0] // TILE
     return pl.pallas_call(
         factor_kernel,
         out_shape=(
             jax.ShapeDtypeStruct(residual.shape, jnp.float32),
             jax.ShapeDtypeStruct(gram.shape, jnp.float32),
         ),
-        in_specs=[vmem, vmem],
-        out_specs=(vmem, vmem),
-        scratch_shapes=[pltpu.VMEM(gram.shape, jnp.float32), pltpu.VMEM(residual.shape, jnp.float32)],
+        in_specs=[hbm, hbm],
+        out_specs=(hbm, hbm),
+        scratch_shapes=[
+            pltpu.VMEM(gram.shape, jnp.float32),
+            pltpu.VMEM(residual.shape, jnp.float32),
+            pltpu.VMEM(residual.shape, jnp.float32),
+            pltpu.VMEM(gram.shape, jnp.float32),
+            pltpu.SemaphoreType.DMA((3,)),
+            pltpu.SemaphoreType.DMA((copies,)),
+        ],
         name="factor_and_solve",
     )(gram, residual)
 

time: 105 us -> 101 us (0.962)
  Pallas kernels: 103 us -> 99.1 us
    pallas_call x1, Pallas kernels: 19.9 us -> 16.9 us  [factor_and_solve(): pl.pallas_call(factor_kernel, out_shape=(jax.ShapeDtypeStruct(residual.sh...]
    pallas_call x1, Pallas kernels: 83.5 us -> 82.2 us  [orthogonalize(): pl.pallas_call(functools.partial(orthogonalize_kernel, plan, sizes, weigh...]
where the time goes in v5:
time: 101 us
  Pallas kernels  99.1 us (98%)
  between operations  1.46 us (1%)
    pallas_call x1, Pallas kernels, orthogonalize(): pl.pallas_call(functools.partial(orthogonalize_kernel, plan, sizes, weigh...  82.2 us
    pallas_call x1, Pallas kernels, factor_and_solve(): pl.pallas_call(factor_kernel, out_shape=(jax.ShapeDtypeStruct(residual.sh...  16.9 us

profile of v5, /device:TPU:1, one launch (start us, length us, event | category | flops | bytes accessed | tf_op | source)
XLA Modules:
  0.0 100.6 jit_solution(2558111249200294191)
XLA Ops:
  1.3 82.2 %orthogonalize.1 = (f32[256,512]{1,0:T(8,128)}, f32[512,512]{1,0:T(8,128)}) custom-call(s32[1,1]{1,0:T(1,128)S(6)} %copy.5.counts_ref, f32[256,1024]{1,0:T(8,128)} %basis_hbm.1, f32[256,512]{1,0:T(8,128)} %block_hbm.1), custom_call_target="tpu_custom_call" | custom-call | tf_op jit(solution)/shard_map/orthogonalize/pallas_call | solution.py:454
  83.5 16.9 %factor_and_solve.1 = (f32[256,512]{1,0:T(8,128)}, f32[512,512]{1,0:T(8,128)}) custom-call(f32[512,512]{1,0:T(8,128)} %get-tuple-element.4.gram_hbm, f32[256,512]{1,0:T(8,128)} %get-tuple-element.5.residual_hbm), custom_call_target="tpu_custom_call" | custom-call | tf_op jit(solution)/shard_map/factor_and_solve/pallas_call | solution.py:618

commit v6 on v5

--- a/solution.py
+++ b/solution.py
@@ -32,6 +32,19 @@
 FIRST_ORDER = (0, 1, 2, 3, 1, 0, 4, 5, 3, 2, 1, 0, 6, 7, 5, 4, 3, 2, 1, 0, 7, 6, 5, 4, 3, 2, 1, 0, 7, 6, 5, 4, 3, 2, 1, 0, 7, 6, 5, 4, 3, 2, 1, 0, 7, 6, 5, 4, 3, 2, 1, 0, -1, -2, 7, 6, 5, 4, 3, 2, -3, -4, -5, -6, 7, 6, -7, -8)
 SECOND_ROUTES = ("pz", "zp")
 SECOND_ORDER = (0, 1, 0, 1, 0, 1, 1, 0, 0, 1, 0, -1, 1, -2)
+
+
+def split(value):
+    high = value.astype(jnp.bfloat16)
+    return high, (value - high.astype(jnp.float32)).astype(jnp.bfloat16)
+
+
+def split_product(left_high, left_low, right):
+    def product(left, right):
+        return jnp.dot(left, right, preferred_element_type=jnp.float32)
+
+    high, low = split(right)
+    return product(left_low, high) + product(left_high, low) + product(left_high, high)
 
 
 def plane_sides(chips):
@@ -113,6 +126,7 @@
     coeffs_tiles,
     gram_tiles,
     operator,
+    basis_parts,
     correction,
     residual,
     send_sem,
@@ -322,13 +336,13 @@
         whole = jnp.concatenate([top, jnp.concatenate([top[:, middle:].T, corner], axis=1)], axis=0)
         unit = lax.broadcasted_iota(jnp.int32, whole.shape, 0) == lax.broadcasted_iota(jnp.int32, whole.shape, 1)
         window = slice(index * block, (index + 1) * block)
-        operator[window, window] = jnp.where(unit, 1.0, 0.0) - whole
+        operator[0, window, window], operator[1, window, window] = split(jnp.where(unit, 1.0, 0.0) - whole)
 
     def put_square(owner, offset, left, right):
         whole = -square_at(basis_gram_tiles.at[owner], offset, block, block)
         rows, cols = slice(left * block, (left + 1) * block), slice(right * block, (right + 1) * block)
-        operator[rows, cols] = whole
-        operator[cols, rows] = whole.T
+        operator[0, rows, cols], operator[1, rows, cols] = split(whole)
+        operator[0, cols, rows], operator[1, cols, rows] = split(whole.T)
 
     def consume_diagonals():
         offset = basis_gram[0].offset
@@ -341,6 +355,8 @@
             put_square(owner, piece.offset, left, right)
 
     def produce_coeffs(index):
+        if index == 3:
+            basis_parts[0], basis_parts[1] = split(basis_all[...])
         return pieces_to_tiles(
             transposed_product(basis_all[:, index * block : (index + 1) * block], block_half[...]) * weight
         )
@@ -349,7 +365,7 @@
         piece = coeffs[index]
         value = square_at(coeffs_tiles, piece.offset, block, half)
         window = slice(index * block, (index + 1) * block)
-        change = matrix_product(operator[:, window], value)
+        change = split_product(operator[0, :, window], operator[1, :, window], value)
         removed = matrix_product(basis_all[:, window], value)
         if index == 0:
             correction[...] = change
@@ -387,7 +403,7 @@
 
     run(basis_gram + coeffs, FIRST_ORDER)
 
-    residual[core] -= matrix_product(basis_all[...], correction[...])
+    residual[core] -= split_product(basis_parts[0], basis_parts[1], correction[...])
     stores = [
         pltpu.make_async_copy(
             residual.at[owner, mine],
@@ -473,7 +489,8 @@
             tiles(2, total(basis_gram)),
             tiles(total(coeffs)),
             tiles(2, total(gram)),
-            pltpu.VMEM((columns, columns), jnp.float32),
+            pltpu.VMEM((2, columns, columns), jnp.bfloat16),
+            pltpu.VMEM((2, 2 * slots, columns), jnp.bfloat16),
             pltpu.VMEM((columns, half), jnp.float32),
             pltpu.VMEM((2, 2 * slots, half), jnp.float32),
             pltpu.SemaphoreType.DMA((place["copy"],)),

time: 101 us -> 96.2 us (0.952)
  Pallas kernels: 99.1 us -> 94.5 us
    pallas_call x1, Pallas kernels: 82.2 us -> 77.6 us  [orthogonalize(): pl.pallas_call(functools.partial(orthogonalize_kernel, plan, sizes, weigh...]
where the time goes in v6:
time: 96.2 us; the launch traced here: 96 us
  Pallas kernels  94.5 us (98%)
  between operations  1.46 us (2%)
    pallas_call x1, Pallas kernels, orthogonalize(): pl.pallas_call(functools.partial(orthogonalize_kernel, plan, sizes, weigh...  77.6 us
    pallas_call x1, Pallas kernels, factor_and_solve(): pl.pallas_call(factor_kernel, out_shape=(jax.ShapeDtypeStruct(residual.sh...  16.9 us

profile of v6, /device:TPU:1, one launch (start us, length us, event | category | flops | bytes accessed | tf_op | source)
XLA Modules:
  0.0 96.0 jit_solution(8114071559456144609)
XLA Ops:
  1.3 77.6 %orthogonalize.1 = (f32[256,512]{1,0:T(8,128)}, f32[512,512]{1,0:T(8,128)}) custom-call(s32[1,1]{1,0:T(1,128)S(6)} %copy.5.counts_ref, f32[256,1024]{1,0:T(8,128)} %basis_hbm.1, f32[256,512]{1,0:T(8,128)} %block_hbm.1), custom_call_target="tpu_custom_call" | custom-call | tf_op jit(solution)/shard_map/orthogonalize/pallas_call | solution.py:470
  78.9 16.9 %factor_and_solve.1 = (f32[256,512]{1,0:T(8,128)}, f32[512,512]{1,0:T(8,128)}) custom-call(f32[512,512]{1,0:T(8,128)} %get-tuple-element.4.gram_hbm, f32[256,512]{1,0:T(8,128)} %get-tuple-element.5.residual_hbm), custom_call_target="tpu_custom_call" | custom-call | tf_op jit(solution)/shard_map/factor_and_solve/pallas_call | solution.py:635

commit v7 on v6

--- a/solution.py
+++ b/solution.py
@@ -45,6 +45,19 @@
 
     high, low = split(right)
     return product(left_low, high) + product(left_high, low) + product(left_high, high)
+
+
+def split_fully(value):
+    high = value.astype(jnp.bfloat16)
+    return (high,) + split(value - high.astype(jnp.float32))
+
+
+def full_product(left, right, left_axis):
+    def product(a, b):
+        return lax.dot_general(a, b, (((left_axis,), (0,)), ((), ())), preferred_element_type=jnp.float32)
+
+    small = product(left[1], right[1]) + (product(left[0], right[2]) + product(left[2], right[0]))
+    return small + (product(left[0], right[1]) + product(left[1], right[0])) + product(left[0], right[0])
 
 
 def plane_sides(chips):
@@ -127,6 +140,7 @@
     gram_tiles,
     operator,
     basis_parts,
+    block_parts,
     correction,
     residual,
     send_sem,
@@ -310,7 +324,8 @@
     first, second = 2 * core, 2 * core + 1
 
     def basis_product(left, right):
-        return transposed_product(basis_all[:, lanes(left, block)], basis_all[:, lanes(right, block)]) * weight
+        left, right = ([basis_parts[i, :, lanes(side, block)] for i in range(3)] for side in (left, right))
+        return full_product(left, right, 0) * weight
 
     def upper_tiles(value):
         middle = value.shape[0] // 2
@@ -355,10 +370,9 @@
             put_square(owner, piece.offset, left, right)
 
     def produce_coeffs(index):
-        if index == 3:
-            basis_parts[0], basis_parts[1] = split(basis_all[...])
+        window = slice(index * block, (index + 1) * block)
         return pieces_to_tiles(
-            transposed_product(basis_all[:, index * block : (index + 1) * block], block_half[...]) * weight
+            full_product([basis_parts[i, :, window] for i in range(3)], [block_parts[i] for i in range(3)], 0) * weight
         )
 
     def consume_coeffs(index):
@@ -366,7 +380,7 @@
         value = square_at(coeffs_tiles, piece.offset, block, half)
         window = slice(index * block, (index + 1) * block)
         change = split_product(operator[0, :, window], operator[1, :, window], value)
-        removed = matrix_product(basis_all[:, window], value)
+        removed = full_product([basis_parts[i, :, window] for i in range(3)], split_fully(value), 1)
         if index == 0:
             correction[...] = change
             residual[core] = block_half[...] - removed
@@ -380,13 +394,22 @@
         piece.out, piece.shared = coeffs_tiles, False
     for piece in gram:
         piece.out, piece.shared = gram_tiles.at[core], True
+    def take_basis(side):
+        place = pl.ds(pl.multiple_of(side * wide, TILE), wide)
+        for i, part in enumerate(split_fully(basis_all[:, place])):
+            basis_parts[i, :, place] = part
+
     def produce_diagonals():
         shared[0].wait_recv()
+        take_basis(core)
         return upper_tiles(basis_product(first, first)) + upper_tiles(basis_product(second, second))
 
     def produce_beyond():
         shared[1].wait_recv()
         shared[2].wait_recv()
+        take_basis(1 - core)
+        for i, part in enumerate(split_fully(block_half[...])):
+            block_parts[i] = part
         return pieces_to_tiles(basis_product(second, lax.rem(second + 1, 4)))
 
     basis_gram[0].produce = produce_diagonals
@@ -421,7 +444,7 @@
         for copy in stores:
             copy.start()
         left = residual[0, :, lanes(core, half // 2)]
-        return pieces_to_tiles(transposed_product(left, residual[1]) * weight)
+        return pieces_to_tiles(full_product(split_fully(left), split_fully(residual[1]), 0) * weight)
 
     def consume_corners():
         for owner in range(2):
@@ -437,7 +460,9 @@
                 gram_tiles.at[owner], gram[1].offset, middle, half
             )
 
-    gram[0].produce = lambda: upper_tiles(transposed_product(residual[core], residual[core]) * weight)
+    gram[0].produce = lambda: upper_tiles(
+        full_product(split_fully(residual[core]), split_fully(residual[core]), 0) * weight
+    )
     gram[0].consume = consume_corners
     gram[1].produce = produce_cross
     gram[1].consume = consume_cross
@@ -490,7 +515,8 @@
             tiles(total(coeffs)),
             tiles(2, total(gram)),
             pltpu.VMEM((2, columns, columns), jnp.bfloat16),
-            pltpu.VMEM((2, 2 * slots, columns), jnp.bfloat16),
+            pltpu.VMEM((3, 2 * slots, columns), jnp.bfloat16),
+            pltpu.VMEM((3, 2 * slots, half), jnp.bfloat16),
             pltpu.VMEM((columns, half), jnp.float32),
             pltpu.VMEM((2, 2 * slots, half), jnp.float32),
             pltpu.SemaphoreType.DMA((place["copy"],)),

time: 96.2 us -> 95.6 us (level)
  no operation moved by 1% of the time
where the time goes in v7:
time: 95.6 us; the launch traced here: 95.5 us
  Pallas kernels  94 us (98%)
  between operations  1.44 us (2%)
    pallas_call x1, Pallas kernels, orthogonalize(): pl.pallas_call(functools.partial(orthogonalize_kernel, plan, sizes, weigh...  77.3 us
    pallas_call x1, Pallas kernels, factor_and_solve(): pl.pallas_call(factor_kernel, out_shape=(jax.ShapeDtypeStruct(residual.sh...  16.7 us

profile of v7, /device:TPU:1, one launch (start us, length us, event | category | flops | bytes accessed | tf_op | source)
XLA Modules:
  0.0 95.5 jit_solution(12857628748560333850)
XLA Ops:
  1.3 77.3 %orthogonalize.1 = (f32[256,512]{1,0:T(8,128)}, f32[512,512]{1,0:T(8,128)}) custom-call(s32[1,1]{1,0:T(1,128)S(6)} %copy.5.counts_ref, f32[256,1024]{1,0:T(8,128)} %basis_hbm.1, f32[256,512]{1,0:T(8,128)} %block_hbm.1), custom_call_target="tpu_custom_call" | custom-call | tf_op jit(solution)/shard_map/orthogonalize/pallas_call | solution.py:495
  78.6 16.7 %factor_and_solve.1 = (f32[256,512]{1,0:T(8,128)}, f32[512,512]{1,0:T(8,128)}) custom-call(f32[512,512]{1,0:T(8,128)} %get-tuple-element.4.gram_hbm, f32[256,512]{1,0:T(8,128)} %get-tuple-element.5.residual_hbm), custom_call_target="tpu_custom_call" | custom-call | tf_op jit(solution)/shard_map/factor_and_solve/pallas_call | solution.py:661
